TPU v7x, 128 devices: a whole 4x4x4 slice. The times are simulated.
128 devices in a mesh: row: 8 (over y, z_hi), col: 16 (over x, z_lo, core).
Axes of the slice: x: 4, y: 4, z: 4 (z_hi: 2, z_lo: 2; z = z_hi * 2 + z_lo), core: 2. Of those that a mesh axis runs over, the one named last changes fastest.
Arguments:
- adjacency: bfloat16 [32768, 32768], P('row', 'col'), as said below
- tile_mask: int32 [256, 256], P('row', 'col'), may hold values from 0 to 1, as said below
- out_grad: bfloat16 [32768, 256], P(('row', 'col')), may hold values from -6 to 6
- pre_two: bfloat16 [32768, 256], P(('row', 'col')), may hold values from -6 to 6
- hidden: bfloat16 [32768, 256], P(('col', 'row')), may hold values from -24 to 24
- pre_one: bfloat16 [32768, 256], P(('col', 'row')), may hold values from -6 to 6
- features: bfloat16 [32768, 256], P(('row', 'col')), may hold values from -6 to 6
- w_two: bfloat16 [256, 256], replicated, may hold values from -0.375 to 0.375
- w_one: bfloat16 [256, 256], replicated, may hold values from -0.375 to 0.375
Outputs:
- node_grad: bfloat16 [32768, 256], P(('row', 'col'))
- weight_grad_one: float32 [256, 256], replicated
- weight_grad_two: float32 [256, 256], replicated
Inputs may be any that keep to these rules, and one draw needn't show every extreme that they name: adjacency is symmetric and nonnegative. tile_mask is symmetric and every diagonal tile is 1.
All inputs are finite; a program needn't handle non-finite values.
Results may differ from a plain program's by a relative error of at most 0.02.
Values may be sent and summed in bfloat16 or wider, within the bound.
A program may use at most 128 MiB of HBM per device.

v0:
```python
import jax
import jax.numpy as jnp
from jax import lax
from jax.sharding import PartitionSpec as P


def tile_pick(count, tile_size, tile_total):
    node_ids = lax.broadcasted_iota(jnp.int32, (count, 1), 0)
    tile_ids = lax.broadcasted_iota(jnp.int32, (1, tile_total), 1)
    return (node_ids // tile_size == tile_ids).astype(jnp.bfloat16)


def local(adjacency, tile_mask, out_grad, pre_two, hidden, pre_one, features, w_two, w_one):
    tile_rows, tile_cols = tile_mask.shape
    tile_size = adjacency.shape[0] // tile_rows
    mask_values = tile_mask.astype(jnp.bfloat16)
    shard_nodes = out_grad.shape[0]
    weight_scale = 4.0 * shard_nodes ** (-0.5)
    contract_rows = (((0,), (0,)), ((), ()))
    contract_cols = (((1,), (1,)), ((), ()))
    grad_two = jnp.where(pre_two > 0, out_grad, jnp.zeros_like(out_grad))
    shard_rows = lax.all_gather(grad_two, "col", axis=0, tiled=True)
    count = shard_rows.shape[0]
    strip_rows = adjacency
    picker = tile_pick(count, tile_size, tile_rows)
    strip_mask = jnp.dot(picker, mask_values, preferred_element_type=jnp.float32).astype(
        jnp.bfloat16
    )
    strip_rows = (strip_rows.reshape(count, tile_cols, tile_size) * strip_mask[:, :, None]).reshape(
        count, adjacency.shape[1]
    )
    column_part = lax.dot_general(
        strip_rows, shard_rows, contract_rows, preferred_element_type=jnp.float32
    )
    column_part = column_part.astype(jnp.bfloat16).astype(jnp.float32)
    prop_two = lax.psum_scatter(
        column_part.astype(jnp.bfloat16), "row", scatter_dimension=0, tiled=True
    )
    back_grad = lax.dot_general(prop_two, w_two, contract_cols, preferred_element_type=jnp.float32)
    grad_one = jnp.where(pre_one > 0, back_grad, jnp.zeros_like(back_grad)).astype(jnp.bfloat16)
    shard_rows = lax.all_gather(grad_one, "row", axis=0, tiled=True)
    count = shard_rows.shape[0]
    strip_cols = adjacency
    picker = tile_pick(count, tile_size, tile_cols)
    strip_mask = lax.dot_general(
        mask_values, picker, contract_cols, preferred_element_type=jnp.float32
    ).astype(jnp.bfloat16)
    strip_cols = (strip_cols.reshape(tile_rows, tile_size, count) * strip_mask[:, None, :]).reshape(
        adjacency.shape[0], count
    )
    row_part = jnp.dot(strip_cols, shard_rows, preferred_element_type=jnp.float32)
    term_two = lax.dot_general(hidden, prop_two, contract_rows, preferred_element_type=jnp.float32)
    summed_two = lax.psum(term_two, ("row", "col"))
    row_part = row_part.astype(jnp.bfloat16).astype(jnp.float32)
    prop_one = lax.psum_scatter(
        row_part.astype(jnp.bfloat16), "col", scatter_dimension=0, tiled=True
    )
    term_one = lax.dot_general(
        features, prop_one, contract_rows, preferred_element_type=jnp.float32
    )
    node_grad = lax.dot_general(
        prop_one, w_one, contract_cols, preferred_element_type=jnp.float32
    ).astype(jnp.bfloat16)
    summed_one = lax.psum(term_one, ("row", "col"))
    return (node_grad, summed_one * weight_scale, summed_two * weight_scale)


def solution(mesh):
    return jax.shard_map(
        local,
        mesh=mesh,
        in_specs=(
            P("row", "col"),
            P("row", "col"),
            P(("row", "col"), None),
            P(("row", "col"), None),
            P(("col", "row"), None),
            P(("col", "row"), None),
            P(("row", "col"), None),
            P(),
            P(),
        ),
        out_specs=(P(("row", "col"), None), P(), P()),
        check_vma=False,
    )
```

profile of v0, /device:TPU:1, one launch (start us, length us, event | category | flops | bytes accessed | tf_op | source)
XLA Modules:
  0.0 437.8 jit_solution(10373811274106707431)
XLA Ops:
  7.2 0.0 copy-start
  7.2 0.0 all-gather.3.cloned.1.call-start
  7.2 1.7 compare_select_fusion
  8.9 0.0 all-gather.3.cloned.1.call-update
  8.9 0.0 reduce-scatter.3.cloned.1.call-start
  9.0 0.9 convolution_convert_fusion.1
  9.9 0.5 copy.15
  10.4 37.4 %all-gather.3.cloned.1.call-done = bf16[4096,256]{1,0:T(8,128)(2,1)} async-done(((bf16[256,256]{1,0:T(8,128)(2,1)}), bf16[4096,256]{1,0:T(8,128)(2,1)}) %all-gather.3.cloned.1.call-update) | async-done | bytes 2097168 | tf_op jit(solution)/shard_map/all_gather | solution.py:22
  47.7 0.0 copy-start.7
  47.7 18.8 %mul.31 = bf16[4096,16,128]{2,1,0:T(8,128)(2,1)} broadcast(bf16[4096,16]{1,0:T(8,128)(2,1)S(1)} %copy.15), dimensions={0,1} | broadcast | bytes 16908288 | tf_op jit(solution)/shard_map/mul | solution.py:29
  66.5 0.0 copy-done.7
  66.5 0.0 copy-start.3
  66.5 0.0 copy-start.6
  66.5 14.3 %fusion.2 = bf16[2048,256]{1,0:T(8,128)(2,1)} fusion(bf16[4096,256]{1,0:T(8,128)(2,1)S(1)} %copy-done.7, bf16[4096,2048]{1,0:T(8,128)(2,1)} %param.9, bf16[512,8,16,128]{3,2,1,0:T(8,128)(2,1)} %bitcast.25), kind=kOutput, calls=%fused_computation.6 | convolution fusion | flops 4303880192 | bytes 36700160 | tf_op jit(solution)/shard_map/dot_general | solution.py:32
  80.9 0.0 reduce-scatter.3.cloned.1.call-update
  80.9 0.0 all-gather.5.cloned.1.call-start
  80.9 70.7 %reduce-scatter.3.cloned.1.call-done = bf16[256,256]{1,0:T(8,128)(2,1)} async-done(((bf16[2048,256]{1,0:T(8,128)(2,1)}), bf16[256,256]{1,0:T(8,128)(2,1)}) %reduce-scatter.3.cloned.1.call-update) | async-done | bytes 131088 | tf_op jit(solution)/shard_map/reduce_scatter | solution.py:36
  151.6 0.0 copy-done
  151.6 0.0 copy-done.3
  151.6 1.8 fusion.4
  153.4 0.0 all-gather.5.cloned.1.call-update
  153.4 0.0 reduce-scatter.5.cloned.1.call-start
  153.5 0.0 copy-done.6
  153.5 0.5 fusion.3
  154.0 13.9 %bitcast_multiply_fusion.2 = bf16[4096,2048]{1,0:T(8,128)(2,1)} fusion(bf16[4096,2048]{1,0:T(8,128)(2,1)} %param.9, bf16[32,2048]{1,0:T(8,128)(2,1)S(1)} %fusion.3), kind=kLoop, calls=%fused_computation.3 | loop fusion | flops 8388608 | bytes 33685504 | tf_op jit(solution)/shard_map/mul | solution.py:48
  167.9 0.0 copy-start.1
  167.9 0.0 copy-start.4
  167.9 0.0 copy-start.5
  167.9 0.0 copy-start.2
  167.9 33.0 %all-gather.5.cloned.1.call-done = bf16[2048,256]{1,0:T(8,128)(2,1)} async-done(((bf16[256,256]{1,0:T(8,128)(2,1)}), bf16[2048,256]{1,0:T(8,128)(2,1)}) %all-gather.5.cloned.1.call-update) | async-done | bytes 1048592 | tf_op jit(solution)/shard_map/all_gather | solution.py:41
  201.0 11.9 %convolution_convert_fusion = bf16[4096,256]{1,0:T(8,128)(2,1)} fusion(bf16[4096,2048]{1,0:T(8,128)(2,1)} %bitcast_multiply_fusion.2, bf16[2048,256]{1,0:T(8,128)(2,1)} %all-gather.5.cloned.1.call-done), kind=kOutput, calls=%fused_computation.4 | convolution fusion | flops 4296015872 | bytes 19922944 | tf_op jit(solution)/shard_map/dot_general | solution.py:51
  212.9 0.0 reduce-scatter.5.cloned.1.call-update
  212.9 0.0 all-reduce.3.cloned.1.call-start
  212.9 0.0 copy-done.1
  212.9 0.0 copy-done.4
  213.0 0.9 convolution_bitcast_fusion
  213.9 60.4 %reduce-scatter.5.cloned.1.call-done = bf16[256,256]{1,0:T(8,128)(2,1)} async-done(((bf16[4096,256]{1,0:T(8,128)(2,1)}), bf16[256,256]{1,0:T(8,128)(2,1)}) %reduce-scatter.5.cloned.1.call-update) | async-done | bytes 131088 | tf_op jit(solution)/shard_map/reduce_scatter | solution.py:55
  274.3 0.0 copy-done.5
  274.3 1.8 convolution_bitcast_fusion.1
  276.2 0.0 all-reduce.3.cloned.1.call-update
  276.2 0.0 copy-done.2
  276.2 1.8 convolution_convert_fusion.3
  278.0 150.5 %all-reduce.3.cloned.1.call-done = (f32[256,256]{0,1:T(8,128)}, f32[256,256]{0,1:T(8,128)}) async-done(((f32[256,256]{0,1:T(8,128)}, f32[256,256]{0,1:T(8,128)}), (f32[256,256]{0,1:T(8,128)}, f32[256,256]{0,1:T(8,128)})) %all-reduce.3.cloned.1.call-update) | async-done | bytes 524304 | tf_op jit(solution)/shard_map/psum | solution.py:64
  428.5 1.1 broadcast_multiply_fusion
  429.6 0.8 copy.16
  430.4 0.8 copy.17
  (2 shorter events, 0.0 us)
Async XLA Ops:
  7.2 144.5 %copy-start = (bf16[256,256]{1,0:T(8,128)(2,1)S(1)}, bf16[256,256]{1,0:T(8,128)(2,1)}, u32[]{:S(2)}) copy-start(bf16[256,256]{1,0:T(8,128)(2,1)} %param.16) | copy-start | bytes 393220
  7.2 40.5 %all-gather.3.cloned.1.call-start = ((), (), s32[]{:S(2)}) async-start(), calls=%async_computation.2 | async-start | bytes 2228224 | tf_op jit(solution)/shard_map/all_gather | solution.py:22
  8.9 142.7 %reduce-scatter.3.cloned.1.call-start = ((), (), s32[]{:S(2)}) async-start(), calls=%async_computation.3 | async-start | bytes 1179648 | tf_op jit(solution)/shard_map/reduce_scatter | solution.py:36
  47.7 18.8 %copy-start.7 = (bf16[4096,256]{1,0:T(8,128)(2,1)S(1)}, bf16[4096,256]{1,0:T(8,128)(2,1)}, u32[]{:S(2)}) copy-start(bf16[4096,256]{1,0:T(8,128)(2,1)} %all-gather.3.cloned.1.call-done) | copy-start | bytes 6291460
  66.5 85.1 %copy-start.3 = (bf16[256,256]{1,0:T(8,128)(2,1)S(1)}, bf16[256,256]{1,0:T(8,128)(2,1)}, u32[]{:S(2)}) copy-start(bf16[256,256]{1,0:T(8,128)(2,1)} %param.14) | copy-start | bytes 393220
  66.5 87.0 %copy-start.6 = (s32[32,16]{0,1:T(8,128)S(1)}, s32[32,16]{0,1:T(8,128)}, u32[]{:S(2)}) copy-start(s32[32,16]{0,1:T(8,128)} %param.10) | copy-start | bytes 6148
  80.9 120.1 %all-gather.5.cloned.1.call-start = ((), (), s32[]{:S(2)}) async-start(), calls=%async_computation.4 | async-start | bytes 1179648 | tf_op jit(solution)/shard_map/all_gather | solution.py:41
  153.4 120.9 %reduce-scatter.5.cloned.1.call-start = ((), (), s32[]{:S(2)}) async-start(), calls=%async_computation.5 | async-start | bytes 2228224 | tf_op jit(solution)/shard_map/reduce_scatter | solution.py:55
  167.9 45.0 %copy-start.1 = (bf16[256,256]{1,0:T(8,128)(2,1)S(1)}, bf16[256,256]{1,0:T(8,128)(2,1)}, u32[]{:S(2)}) copy-start(bf16[256,256]{1,0:T(8,128)(2,1)} %reduce-scatter.3.cloned.1.call-done) | copy-start | bytes 393220
  167.9 45.0 %copy-start.4 = (bf16[256,256]{1,0:T(8,128)(2,1)S(1)}, bf16[256,256]{1,0:T(8,128)(2,1)}, u32[]{:S(2)}) copy-start(bf16[256,256]{1,0:T(8,128)(2,1)} %param.13) | copy-start | bytes 393220
  167.9 106.4 %copy-start.5 = (bf16[256,256]{1,0:T(8,128)(2,1)S(1)}, bf16[256,256]{1,0:T(8,128)(2,1)}, u32[]{:S(2)}) copy-start(bf16[256,256]{1,0:T(8,128)(2,1)} %param.15) | copy-start | bytes 393220
  167.9 108.2 %copy-start.2 = (bf16[256,256]{1,0:T(8,128)(2,1)S(1)}, bf16[256,256]{1,0:T(8,128)(2,1)}, u32[]{:S(2)}) copy-start(bf16[256,256]{1,0:T(8,128)(2,1)} %param.17) | copy-start | bytes 393220
  212.9 215.6 %all-reduce.3.cloned.1.call-start = ((), (), s32[]{:S(2)}) async-start(), calls=%async_computation.6 | async-start | bytes 1048576 | tf_op jit(solution)/shard_map/psum | solution.py:64
Sparse Core Ops, SparseCore 0:
  10.3 37.4 all-gather.2
  81.0 70.5 reduce-scatter.2
  154.5 46.3 all-gather.4
  213.0 61.2 reduce-scatter.4
  279.7 148.7 all-reduce.2
where the time goes:
time: 438 us
  waiting for transfers between devices  352 us (80%)
  matrix products  33.9 us (8%)
  local copies, waits for them, and re-layouts  21 us (5%)
  other arithmetic  16.7 us (4%)
  between operations  13.9 us (3%)
    psum x1, waiting for transfers between devices, local(): summed_one = lax.psum(term_one, ('row', 'col'))  151 us
    reduce_scatter x1, waiting for transfers between devices, local(): lax.psum_scatter(column_part.astype(jnp.bfloat16), 'row', scatter_dimensi...  70.7 us
    reduce_scatter x1, waiting for transfers between devices, local(): lax.psum_scatter(row_part.astype(jnp.bfloat16), 'col', scatter_dimension=...  60.4 us
    all_gather x1, waiting for transfers between devices, local(): shard_rows = lax.all_gather(grad_two, 'col', axis=0, tiled=True)  37.4 us
    all_gather x1, waiting for transfers between devices, local(): shard_rows = lax.all_gather(grad_one, 'row', axis=0, tiled=True)  33 us
    mul x1, local copies, waits for them, and re-layouts, local(): strip_rows.reshape(count, tile_cols, tile_size) * strip_mask[:, :, None]  18.8 us
    dot_general x1, matrix products, local(): lax.dot_general(strip_rows, shard_rows, contract_rows, preferred_element_...  14.3 us
    mul x1, other arithmetic, local(): strip_cols.reshape(tile_rows, tile_size, count) * strip_mask[:, None, :]  13.9 us
  transfers between devices with their start and end apart: 5, of which 5 were waited for; matrix products, arithmetic and copies ran while one was open for 4% of the time, Pallas kernels for 0%

commit v1 on v0

--- a/solution.py
+++ b/solution.py
@@ -2,6 +2,15 @@
 import jax.numpy as jnp
 from jax import lax
 from jax.sharding import PartitionSpec as P
+from jax.lax import psum
+
+
+def find_the_area(inp):
+    ax_name = "row"
+    mesh_name = "col"
+    for dd in (mesh_name, ax_name):
+        inp = psum(inp, dd)
+    return inp
 
 
 def tile_pick(count, tile_size, tile_total):
@@ -61,7 +70,7 @@
     node_grad = lax.dot_general(
         prop_one, w_one, contract_cols, preferred_element_type=jnp.float32
     ).astype(jnp.bfloat16)
-    summed_one = lax.psum(term_one, ("row", "col"))
+    summed_one = find_the_area(term_one)
     return (node_grad, summed_one * weight_scale, summed_two * weight_scale)
 
 

time: 438 us -> 640 us (1.46)
  waiting for transfers between devices: 352 us -> 548 us
    psum x1 -> x3, waiting for transfers between devices: 151 us -> 345 us  [the longest x2 196 us: find_the_area(): inp = psum(inp, dd)]
  transfers between devices with their start and end apart: 5 -> 7, of which waited for: 5 -> 7; matrix products, arithmetic and copies ran while one was open for 4% -> 3% of each run, Pallas kernels for 0% -> 0%
where the time goes in v1:
time: 640 us; the launch traced here: 634 us
  waiting for transfers between devices  548 us (86%)
  matrix products  33.9 us (5%)
  local copies, waits for them, and re-layouts  21 us (3%)
  other arithmetic  17.5 us (3%)
  between operations  14.2 us (2%)
    psum x2, waiting for transfers between devices, find_the_area(): inp = psum(inp, dd)  196 us
    psum x1, waiting for transfers between devices, local(): summed_two = lax.psum(term_two, ('row', 'col'))  149 us
    reduce_scatter x1, waiting for transfers between devices, local(): lax.psum_scatter(column_part.astype(jnp.bfloat16), 'row', scatter_dimensi...  70.6 us
    reduce_scatter x1, waiting for transfers between devices, local(): lax.psum_scatter(row_part.astype(jnp.bfloat16), 'col', scatter_dimension=...  61.5 us
    all_gather x1, waiting for transfers between devices, local(): shard_rows = lax.all_gather(grad_two, 'col', axis=0, tiled=True)  37.4 us
    all_gather x1, waiting for transfers between devices, local(): shard_rows = lax.all_gather(grad_one, 'row', axis=0, tiled=True)  33 us
    mul x1, local copies, waits for them, and re-layouts, local(): strip_rows.reshape(count, tile_cols, tile_size) * strip_mask[:, :, None]  18.8 us
    dot_general x1, matrix products, local(): lax.dot_general(strip_rows, shard_rows, contract_rows, preferred_element_...  14.3 us
  transfers between devices with their start and end apart: 7, of which 7 were waited for; matrix products, arithmetic and copies ran while one was open for 3% of the time, Pallas kernels for 0%

profile of v1, /device:TPU:1, one launch (start us, length us, event | category | flops | bytes accessed | tf_op | source)
XLA Modules:
  0.0 634.4 jit_solution(17752263189853147945)
XLA Ops:
  7.2 0.0 copy-start
  7.2 0.0 all-gather.3.cloned.1.call-start
  7.2 1.7 compare_select_fusion
  8.9 0.0 all-gather.3.cloned.1.call-update
  8.9 0.0 reduce-scatter.3.cloned.1.call-start
  9.0 0.9 convolution_convert_fusion.1
  9.9 0.5 copy.15
  10.4 37.4 %all-gather.3.cloned.1.call-done = bf16[4096,256]{1,0:T(8,128)(2,1)} async-done(((bf16[256,256]{1,0:T(8,128)(2,1)}), bf16[4096,256]{1,0:T(8,128)(2,1)}) %all-gather.3.cloned.1.call-update) | async-done | bytes 2097168 | tf_op jit(solution)/shard_map/all_gather | solution.py:31
  47.7 0.0 copy-start.7
  47.7 18.8 %mul.31 = bf16[4096,16,128]{2,1,0:T(8,128)(2,1)} broadcast(bf16[4096,16]{1,0:T(8,128)(2,1)S(1)} %copy.15), dimensions={0,1} | broadcast | bytes 16908288 | tf_op jit(solution)/shard_map/mul | solution.py:38
  66.5 0.0 copy-done.7
  66.5 0.0 copy-start.3
  66.5 0.0 copy-start.6
  66.5 14.3 %fusion.2 = bf16[2048,256]{1,0:T(8,128)(2,1)} fusion(bf16[4096,256]{1,0:T(8,128)(2,1)S(1)} %copy-done.7, bf16[4096,2048]{1,0:T(8,128)(2,1)} %param.9, bf16[512,8,16,128]{3,2,1,0:T(8,128)(2,1)} %bitcast.25), kind=kOutput, calls=%fused_computation.6 | convolution fusion | flops 4303880192 | bytes 36700160 | tf_op jit(solution)/shard_map/dot_general | solution.py:41
  80.8 0.0 reduce-scatter.3.cloned.1.call-update
  80.8 0.0 all-gather.5.cloned.1.call-start
  80.9 70.6 %reduce-scatter.3.cloned.1.call-done = bf16[256,256]{1,0:T(8,128)(2,1)} async-done(((bf16[2048,256]{1,0:T(8,128)(2,1)}), bf16[256,256]{1,0:T(8,128)(2,1)}) %reduce-scatter.3.cloned.1.call-update) | async-done | bytes 131088 | tf_op jit(solution)/shard_map/reduce_scatter | solution.py:45
  151.5 0.0 copy-done
  151.5 0.0 copy-done.3
  151.6 1.8 fusion.4
  153.3 0.0 all-gather.5.cloned.1.call-update
  153.4 0.0 reduce-scatter.5.cloned.1.call-start
  153.4 0.0 copy-done.6
  153.4 0.5 fusion.3
  153.9 13.9 %bitcast_multiply_fusion.2 = bf16[4096,2048]{1,0:T(8,128)(2,1)} fusion(bf16[4096,2048]{1,0:T(8,128)(2,1)} %param.9, bf16[32,2048]{1,0:T(8,128)(2,1)S(1)} %fusion.3), kind=kLoop, calls=%fused_computation.3 | loop fusion | flops 8388608 | bytes 33685504 | tf_op jit(solution)/shard_map/mul | solution.py:57
  167.9 0.0 copy-start.4
  167.9 0.0 copy-start.1
  167.9 0.0 copy-start.5
  167.9 0.0 copy-start.2
  167.9 33.0 %all-gather.5.cloned.1.call-done = bf16[2048,256]{1,0:T(8,128)(2,1)} async-done(((bf16[256,256]{1,0:T(8,128)(2,1)}), bf16[2048,256]{1,0:T(8,128)(2,1)}) %all-gather.5.cloned.1.call-update) | async-done | bytes 1048592 | tf_op jit(solution)/shard_map/all_gather | solution.py:50
  200.9 11.9 %convolution_convert_fusion = bf16[4096,256]{1,0:T(8,128)(2,1)} fusion(bf16[4096,2048]{1,0:T(8,128)(2,1)} %bitcast_multiply_fusion.2, bf16[2048,256]{1,0:T(8,128)(2,1)} %all-gather.5.cloned.1.call-done), kind=kOutput, calls=%fused_computation.4 | convolution fusion | flops 4296015872 | bytes 19922944 | tf_op jit(solution)/shard_map/dot_general | solution.py:60
  212.8 0.0 reduce-scatter.5.cloned.1.call-update
  212.8 0.0 all-reduce.4.cloned.1.call-start
  212.8 61.5 %reduce-scatter.5.cloned.1.call-done = bf16[256,256]{1,0:T(8,128)(2,1)} async-done(((bf16[4096,256]{1,0:T(8,128)(2,1)}), bf16[256,256]{1,0:T(8,128)(2,1)}) %reduce-scatter.5.cloned.1.call-update) | async-done | bytes 131088 | tf_op jit(solution)/shard_map/reduce_scatter | solution.py:64
  274.4 0.0 copy-done.4
  274.4 1.8 convolution_bitcast_fusion.1
  276.2 0.0 all-reduce.4.cloned.1.call-update
  276.2 0.0 all-reduce.8.cloned.1.call-start
  276.3 0.0 copy-done.1
  276.3 0.0 copy-done.5
  276.3 0.9 convolution_bitcast_fusion
  277.2 0.0 all-reduce.8.cloned.1.call-update
  277.3 0.0 all-reduce.6.cloned.1.call-start
  277.3 119.8 %all-reduce.4.cloned.1.call-done = f32[256,256]{0,1:T(8,128)} async-done(((f32[256,256]{0,1:T(8,128)}), f32[256,256]{0,1:T(8,128)}) %all-reduce.4.cloned.1.call-update) | async-done | bytes 262160 | tf_op jit(solution)/shard_map/psum | solution.py:12
  397.1 0.0 all-reduce.6.cloned.1.call-update
  397.1 149.3 %all-reduce.8.cloned.1.call-done = f32[256,256]{0,1:T(8,128)} async-done(((f32[256,256]{0,1:T(8,128)}), f32[256,256]{0,1:T(8,128)}) %all-reduce.8.cloned.1.call-update) | async-done | bytes 262160 | tf_op jit(solution)/shard_map/psum | solution.py:62
  546.4 1.0 broadcast_multiply_fusion
  547.4 0.8 copy.17
  548.2 0.0 copy-done.2
  548.2 1.8 convolution_convert_fusion.3
  550.0 75.8 %all-reduce.6.cloned.1.call-done = f32[256,256]{0,1:T(8,128)} async-done(((f32[256,256]{0,1:T(8,128)}), f32[256,256]{0,1:T(8,128)}) %all-reduce.6.cloned.1.call-update) | async-done | bytes 262160 | tf_op jit(solution)/shard_map/psum | solution.py:12
  625.8 1.0 broadcast_multiply_fusion.1
  626.8 0.8 copy.16
  (2 shorter events, 0.0 us)
Async XLA Ops:
  7.2 144.4 %copy-start = (bf16[256,256]{1,0:T(8,128)(2,1)S(1)}, bf16[256,256]{1,0:T(8,128)(2,1)}, u32[]{:S(2)}) copy-start(bf16[256,256]{1,0:T(8,128)(2,1)} %param.16) | copy-start | bytes 393220
  7.2 40.5 %all-gather.3.cloned.1.call-start = ((), (), s32[]{:S(2)}) async-start(), calls=%async_computation.2 | async-start | bytes 2228224 | tf_op jit(solution)/shard_map/all_gather | solution.py:31
  8.9 142.6 %reduce-scatter.3.cloned.1.call-start = ((), (), s32[]{:S(2)}) async-start(), calls=%async_computation.3 | async-start | bytes 1179648 | tf_op jit(solution)/shard_map/reduce_scatter | solution.py:45
  47.7 18.8 %copy-start.7 = (bf16[4096,256]{1,0:T(8,128)(2,1)S(1)}, bf16[4096,256]{1,0:T(8,128)(2,1)}, u32[]{:S(2)}) copy-start(bf16[4096,256]{1,0:T(8,128)(2,1)} %all-gather.3.cloned.1.call-done) | copy-start | bytes 6291460
  66.5 85.0 %copy-start.3 = (bf16[256,256]{1,0:T(8,128)(2,1)S(1)}, bf16[256,256]{1,0:T(8,128)(2,1)}, u32[]{:S(2)}) copy-start(bf16[256,256]{1,0:T(8,128)(2,1)} %param.14) | copy-start | bytes 393220
  66.5 86.9 %copy-start.6 = (s32[32,16]{0,1:T(8,128)S(1)}, s32[32,16]{0,1:T(8,128)}, u32[]{:S(2)}) copy-start(s32[32,16]{0,1:T(8,128)} %param.10) | copy-start | bytes 6148
  80.8 120.1 %all-gather.5.cloned.1.call-start = ((), (), s32[]{:S(2)}) async-start(), calls=%async_computation.4 | async-start | bytes 1179648 | tf_op jit(solution)/shard_map/all_gather | solution.py:50
  153.4 121.0 %reduce-scatter.5.cloned.1.call-start = ((), (), s32[]{:S(2)}) async-start(), calls=%async_computation.5 | async-start | bytes 2228224 | tf_op jit(solution)/shard_map/reduce_scatter | solution.py:64
  167.9 106.5 %copy-start.4 = (bf16[256,256]{1,0:T(8,128)(2,1)S(1)}, bf16[256,256]{1,0:T(8,128)(2,1)}, u32[]{:S(2)}) copy-start(bf16[256,256]{1,0:T(8,128)(2,1)} %param.15) | copy-start | bytes 393220
  167.9 108.4 %copy-start.1 = (bf16[256,256]{1,0:T(8,128)(2,1)S(1)}, bf16[256,256]{1,0:T(8,128)(2,1)}, u32[]{:S(2)}) copy-start(bf16[256,256]{1,0:T(8,128)(2,1)} %reduce-scatter.3.cloned.1.call-done) | copy-start | bytes 393220
  167.9 108.4 %copy-start.5 = (bf16[256,256]{1,0:T(8,128)(2,1)S(1)}, bf16[256,256]{1,0:T(8,128)(2,1)}, u32[]{:S(2)}) copy-start(bf16[256,256]{1,0:T(8,128)(2,1)} %param.13) | copy-start | bytes 393220
  167.9 380.3 %copy-start.2 = (bf16[256,256]{1,0:T(8,128)(2,1)S(1)}, bf16[256,256]{1,0:T(8,128)(2,1)}, u32[]{:S(2)}) copy-start(bf16[256,256]{1,0:T(8,128)(2,1)} %param.17) | copy-start | bytes 393220
  212.8 184.3 %all-reduce.4.cloned.1.call-start = ((), (), s32[]{:S(2)}) async-start(), calls=%async_computation.6 | async-start | bytes 524288 | tf_op jit(solution)/shard_map/psum | solution.py:12
  276.2 270.2 %all-reduce.8.cloned.1.call-start = ((), (), s32[]{:S(2)}) async-start(), calls=%async_computation.8 | async-start | bytes 524288 | tf_op jit(solution)/shard_map/psum | solution.py:62
  277.3 348.5 %all-reduce.6.cloned.1.call-start = ((), (), s32[]{:S(2)}) async-start(), calls=%async_computation.7 | async-start | bytes 524288 | tf_op jit(solution)/shard_map/psum | solution.py:12
Sparse Core Ops, SparseCore 0:
  10.3 37.4 all-gather.2
  81.0 70.5 reduce-scatter.2
  154.5 46.3 all-gather.4
  212.9 61.4 reduce-scatter.4
  277.3 119.7 all-reduce.3
  402.3 144.0 all-reduce.7
  548.9 76.8 all-reduce.5
